TPU v7x, 32 devices: a whole 2x2x4 slice. The times are simulated.
32 devices in a mesh: pw: 16 (over z, x, core), ka: 2 (over y).
Axes of the slice: x: 2, y: 2, z: 4, core: 2. Of those that a mesh axis runs over, the one named last changes fastest.
Arguments:
- waves: bfloat16 [2, 2, 32768, 256], P('ka', None, 'pw'), may hold values from -0.125 to 0.125
- projectors: bfloat16 [2, 2, 32768, 2304], P('ka', None, 'pw'), may hold values from -0.125 to 0.125
- projector_order: int32 [2304], replicated, may hold values from 0 to 2303, each once
- shift_map: int32 [32768], P('pw'), may hold values from 0 to 32767, as said below
- charges: float32 [128, 18, 18], replicated, may hold values from -0.125 to 0.125
- atom_phase: float32 [128], replicated, may hold values from -3.140625 to 3.140625
Outputs:
- margins: float32 [2, 256, 2, 256], P('ka', 'pw')
Inputs may be any that keep to these rules, and one draw needn't show every extreme that they name: `projector_order`: each projector slot once. `shift_map`: a permutation of the plane waves that maps every aligned block of 2048 plane waves onto itself.
All inputs are finite; a program needn't handle non-finite values.
Results may differ from a plain program's by a relative error of at most 0.0003.
Values may be sent and summed in bfloat16 or wider, within the bound.
A program may use at most 128 MiB of HBM per device.

v0:
```python
import jax
import jax.numpy as jnp
from jax import lax
from jax.sharding import PartitionSpec as P

PPA = 18


def from_behind(block, axis, distance):
    devices = range(lax.axis_size(axis))
    route = [((i - distance) % len(devices), i) for i in devices]
    return lax.ppermute(block, axis, route)


def contract(left, right, precision=None):
    return lax.dot_general(
        left,
        right,
        (((0,), (0,)), ((), ())),
        precision=precision,
        preferred_element_type=jnp.float32,
    )


def complex_cross(left, right, precision=None):
    real = contract(left[0], right[0], precision) + contract(left[1], right[1], precision)
    imag = contract(left[0], right[1], precision) - contract(left[1], right[0], precision)
    return jnp.stack([real, imag], axis=1)


def rotate(block, phases):
    repeated = jnp.repeat(phases, PPA)
    cosine = jnp.cos(repeated)[:, None]
    sine = jnp.sin(repeated)[:, None]
    return jnp.stack([block[0] * cosine + block[1] * sine, block[1] * cosine - block[0] * sine])


def apply_charges(sym, block):
    atoms = block.shape[1] // PPA
    split = block.reshape(2, atoms, PPA, block.shape[2])
    weighted = jnp.einsum(
        "apq,raqj->rapj",
        sym,
        split,
        precision=lax.Precision.HIGHEST,
        preferred_element_type=jnp.float32,
    )
    return weighted.reshape(block.shape)


def local(waves, projectors, projector_order, shift_map, charges, atom_phase):
    wave = waves[0]
    beta = projectors[0]
    pw_dev = wave.shape[1]
    last_k = lax.axis_index("ka") == lax.axis_size("ka") - 1
    pw_index = lax.axis_index("pw")
    received = from_behind(wave, "ka", -1)
    local_map = shift_map - pw_index * pw_dev
    permuted = jnp.take(received, local_map, axis=1)
    next_wave = jnp.where(last_k, permuted, received)
    real = contract(beta[0], wave[0]) + contract(beta[1], wave[1])
    imag = contract(beta[0], wave[1]) - contract(beta[1], wave[0])
    inverse = jnp.argsort(projector_order)
    sorted_part = jnp.stack([real, imag])[:, inverse, :]
    sym = 0.5 * (charges + jnp.transpose(charges, (0, 2, 1)))
    block = lax.psum_scatter(sorted_part, "pw", scatter_dimension=1, tiled=True)
    next_block = from_behind(block, "ka", -1)
    atom_dev = block.shape[1] // PPA
    own_phase = lax.dynamic_slice_in_dim(atom_phase, pw_index * atom_dev, atom_dev)
    own_sym = lax.dynamic_slice_in_dim(sym, pw_index * atom_dev, atom_dev, 0)
    next_block = jnp.where(last_k, rotate(next_block, own_phase), next_block)
    weighted = apply_charges(own_sym, next_block)
    result = complex_cross(wave, next_wave)
    result = result + complex_cross(block, weighted, lax.Precision.HIGHEST)
    summed = lax.psum_scatter(result, "pw", scatter_dimension=0, tiled=True)
    return summed[None]


def solution(mesh):
    placed = (P("ka", None, "pw", None), P("ka", None, "pw", None), P(), P("pw"), P(), P())
    return jax.shard_map(
        local, mesh=mesh, in_specs=placed, out_specs=P("ka", "pw", None, None), check_vma=False
    )
```

profile of v0, /device:TPU:0, one launch (start us, length us, event | category | flops | bytes accessed | tf_op | source)
XLA Modules:
  0.0 300.1 jit_solution(15753953768008242075)
XLA Ops:
  6.5 6.0 %copy.104 = bf16[1,2,2048,256]{3,1,2,0:T(2,128)(2,1)} copy(bf16[1,2,2048,256]{3,2,1,0:T(8,128)(2,1)} %param.6) | data formatting | bytes 4194304 | tf_op args[0]
  12.5 3.1 %collective-permute-start = (bf16[2,2048,256]{2,0,1:T(2,128)(2,1)}, bf16[2,2048,256]{2,0,1:T(2,128)(2,1)S(1)}, u32[]{:S(2)}, u32[]{:S(2)}) collective-permute-start(bf16[2,2048,256]{2,0,1:T(2,128)(2,1)} %bitcast.96), channel_id=1, source_target_pairs={{1,0},{0,1},{3,2},{2,3},{5,4},{4,5},{7,6},{6,7},{9,8},{8,9},{11,10... | collective-permute-start | bytes 6291464 | tf_op jit(solution)/shard_map/ppermute | solution.py:12
  15.6 6.0 %fusion = f32[2304,256]{1,0:T(8,128)S(1)} fusion(bf16[1,2,2048,2304]{3,2,1,0:T(8,128)(2,1)} %param.7, bf16[1,2,2048,256]{3,2,1,0:T(8,128)(2,1)S(1)} %copy-done), kind=kOutput, calls=%fused_computation.2 | convolution fusion | flops 2415919104 | bytes 12845056 | tf_op jit(solution)/shard_map/dot_general | solution.py:16
  21.7 4.2 %fusion.2 = f32[2304,256]{1,0:T(8,128)} fusion(bf16[1,2,2048,2304]{3,2,1,0:T(8,128)(2,1)S(1)} %bitcast.102, bf16[1,2,2048,256]{3,2,1,0:T(8,128)(2,1)S(1)} %copy-done), kind=kOutput, calls=%fused_computation.4 | convolution fusion | flops 2415919104 | bytes 12845056 | tf_op jit(solution)/shard_map/dot_general | solution.py:16
  25.9 2.8 fusion.18
  28.8 4.5 %fusion.21 = f32[1,2304,256]{2,1,0:T(8,128)S(1)} fusion(f32[2304,256]{1,0:T(8,128)} %fusion.2, bf16[1,2,2048,2304]{3,2,1,0:T(8,128)(2,1)S(1)} %bitcast.102, bf16[1,2,2048,256]{3,2,1,0:T(8,128)(2,1)S(1)} %copy-done), kind=kOutput, calls=%fused_computation.20 | convolution fusion | flops 2416508928 | bytes 15204352 | tf_op jit(solution)/shard_map/dot_general | solution.py:16
  33.6 14.4 %copy.46 = f32[2,2304,256]{2,0,1:T(2,128)} copy(f32[2,2304,256]{2,1,0:T(8,128)S(1)} %pad_maximum_fusion) | data formatting | bytes 9437184 | tf_op jit(solution)/shard_map/stack | solution.py:64
  48.0 5.8 %sort.17 = (s32[2304]{0:T(1024)}, s32[2304]{0:T(1024)S(1)}) sort(s32[2304]{0:T(1024)S(1)} %copy-done.5, s32[2304]{0:T(1024)S(1)} %iota.4), dimensions={0}, to_apply=%region_0.1 | sort | flops 27648 | bytes 36864 | tf_op jit(solution)/shard_map/jit(argsort)/sort | solution.py:63
  53.8 14.2 %gather_fusion.1 = f32[2304,2,256]{2,1,0:T(2,128)} fusion(f32[2,2304,256]{2,0,1:T(2,128)} %copy.46, s32[3072]{0:T(1024)S(1)} %pad_clamp_fusion), kind=kCustom, calls=%fused_computation.1 | custom fusion | bytes 9446400 | tf_op jit(solution)/shard_map/gather | solution.py:64
  70.8 16.7 %gather_fusion = bf16[2048,2,256]{2,1,0:T(2,128)(2,1)} fusion(bf16[2,2048,256]{2,0,1:T(2,128)(2,1)S(1)} %collective-permute-done, s32[2048]{0:T(1024)S(1)} %fusion.67), kind=kCustom, calls=%fused_computation | custom fusion | bytes 4202496 | tf_op jit(solution)/shard_map/jit(_take)/gather | solution.py:59
  87.5 10.2 %broadcast_select_fusion.1 = bf16[2,2048,256]{2,0,1:T(2,128)(2,1)S(1)} fusion(bf16[2,2048,256]{2,0,1:T(2,128)(2,1)S(1)} %collective-permute-done, pred[]{:T(512)S(6)} %eq.3, bf16[2048,2,256]{2,1,0:T(2,128)(2,1)} %gather_fusion, pred[2048]{0:T(1024)(128)(4,1)S(1)} %compare_and_fusion), kind=kLoop, calls=%fused_computation.16 | loop fusion | flops 2097152 | bytes 6293505 | tf_op jit(solution)/shard_map/jit(_where)/select_n | solution.py:60
  97.7 3.0 fusion.68
  102.5 84.1 %all-reduce.5.cloned.1.call-done = f32[2,2304,256]{2,0,1:T(2,128)} async-done(((f32[2,2304,256]{2,0,1:T(2,128)}), f32[2,2304,256]{2,0,1:T(2,128)}) %all-reduce.5.cloned.1.call-update) | async-done | bytes 4718608
  186.6 1.1 constant_dynamic-slice_fusion.2
  187.7 1.5 collective-permute-start.1
  189.3 2.1 fusion.26
  191.3 1.3 constant_dynamic-slice_fusion
  192.6 3.0 collective-permute-done.1
  196.6 0.7 fusion.61
  197.3 0.7 fusion.59
  197.9 0.7 fusion.25
  199.4 1.0 copy.56
  201.0 90.8 %all-reduce.7.cloned.1.call-done = f32[256,2,256]{2,1,0:T(2,128)} async-done(((f32[256,2,256]{2,1,0:T(2,128)}), f32[256,2,256]{2,1,0:T(2,128)}) %all-reduce.7.cloned.1.call-update) | async-done | bytes 524304
  291.9 1.4 dynamic-slice_bitcast_fusion
  (60 shorter events, 5.9 us)
Async XLA Ops:
  6.5 180.1 %all-reduce.5.cloned.1.call-start = ((), (), s32[]{:S(2)}) async-start(), calls=%async_computation | async-start | bytes 9437184
  6.5 9.0 %copy-start = (bf16[1,2,2048,256]{3,2,1,0:T(8,128)(2,1)S(1)}, bf16[1,2,2048,256]{3,2,1,0:T(8,128)(2,1)}, u32[]{:S(2)}) copy-start(bf16[1,2,2048,256]{3,2,1,0:T(8,128)(2,1)} %param.6) | copy-start | bytes 6291460
  6.5 15.1 %slice-start = ((s8[18874368]{0:T(1024)(128)(4,1)}), s8[4194304]{0:T(1024)(128)(4,1)S(1)}, s32[]{:S(2)}) async-start(s8[18874368]{0:T(1024)(128)(4,1)} %bitcast.101), calls=%async_computation.2 | async-start | bytes 8388608
  12.5 9.1 %slice-start.1 = ((s8[18874368]{0:T(1024)(128)(4,1)}), s8[4194304]{0:T(1024)(128)(4,1)S(1)}, s32[]{:S(2)}) async-start(s8[18874368]{0:T(1024)(128)(4,1)} %bitcast.101), calls=%async_computation.3 | async-start | bytes 8388608
  12.5 9.1 %slice-start.2 = ((s8[18874368]{0:T(1024)(128)(4,1)}), s8[4194304]{0:T(1024)(128)(4,1)S(1)}, s32[]{:S(2)}) async-start(s8[18874368]{0:T(1024)(128)(4,1)} %bitcast.101), calls=%async_computation.4 | async-start | bytes 8388608
  12.5 9.2 %slice-start.3 = ((s8[18874368]{0:T(1024)(128)(4,1)}), s8[4194304]{0:T(1024)(128)(4,1)S(1)}, s32[]{:S(2)}) async-start(s8[18874368]{0:T(1024)(128)(4,1)} %bitcast.101), calls=%async_computation.5 | async-start | bytes 8388608
  12.5 9.2 %slice-start.4 = ((s8[18874368]{0:T(1024)(128)(4,1)}), s8[2097152]{0:T(1024)(128)(4,1)S(1)}, s32[]{:S(2)}) async-start(s8[18874368]{0:T(1024)(128)(4,1)} %bitcast.101), calls=%async_computation.6 | async-start | bytes 4194304
  12.5 58.3 %collective-permute-start = (bf16[2,2048,256]{2,0,1:T(2,128)(2,1)}, bf16[2,2048,256]{2,0,1:T(2,128)(2,1)S(1)}, u32[]{:S(2)}, u32[]{:S(2)}) collective-permute-start(bf16[2,2048,256]{2,0,1:T(2,128)(2,1)} %bitcast.96), channel_id=1, source_target_pairs={{1,0},{0,1},{3,2},{2,3},{5,4},{4,5},{7,6},{6,7},{9,8},{8,9},{11,10... | collective-permute-start | bytes 6291464 | tf_op jit(solution)/shard_map/ppermute | solution.py:12
  33.6 14.4 %copy-start.5 = (s32[2304]{0:T(1024)S(1)}, s32[2304]{0:T(1024)}, u32[]{:S(2)}) copy-start(s32[2304]{0:T(1024)} %param.8) | copy-start | bytes 27652
  68.0 0.7 copy-start.6
  68.0 1.1 copy-start.3
  68.0 1.5 copy-start.7
  68.0 2.8 copy-start.4
  68.0 223.8 %all-reduce.7.cloned.1.call-start = ((), (), s32[]{:S(2)}) async-start(), calls=%async_computation.1 | async-start | bytes 1048576
  97.7 3.0 %copy-start.1 = (bf16[1,2,2048,256]{3,2,1,0:T(8,128)(2,1)S(1)}, bf16[1,2,2048,256]{3,2,1,0:T(8,128)(2,1)}, u32[]{:S(2)}) copy-start(bf16[1,2,2048,256]{3,2,1,0:T(8,128)(2,1)} %param.6) | copy-start | bytes 6291460
  100.7 1.3 copy-start.2
  187.7 7.9 %collective-permute-start.1 = (f32[2,144,256]{2,1,0:T(8,128)S(1)}, f32[2,144,256]{2,1,0:T(8,128)S(1)}, u32[]{:S(2)}, u32[]{:S(2)}) collective-permute-start(f32[2,144,256]{2,1,0:T(8,128)S(1)} %copy.47), channel_id=1, source_target_pairs={{1,0},{0,1},{3,2},{2,3},{5,4},{4,5},{7,6},{6,7},{9,8},{8,9},{11,10... | collective-permute-start | bytes 884744 | tf_op jit(solution)/shard_map/ppermute | solution.py:12
Sparse Core Ops, SparseCore 0:
  68.2 118.4 all-reduce.4
  200.5 91.3 all-reduce.6
where the time goes:
time: 301 us; the launch traced here: 300 us
  waiting for transfers between devices  178 us (59%)
  local copies, waits for them, and re-layouts  61.4 us (20%)
  matrix products  24.4 us (8%)
  other arithmetic  16.7 us (6%)
  between operations  15.1 us (5%)
  starting transfers between devices  4.64 us (2%)
    unnamed x4, waiting for transfers between devices  175 us
    dot_general x12, matrix products, contract(): lax.dot_general(left, right, (((0,), (0,)), ((), ())), precision=precisio...  23.9 us
    gather x1, local copies, waits for them, and re-layouts, local(): permuted = jnp.take(received, local_map, axis=1)  16.7 us
    another operation x1, local copies, waits for them, and re-layouts, local(): sorted_part = jnp.stack([real, imag])[:, inverse, :]  14.4 us
    gather x1, local copies, waits for them, and re-layouts, local(): sorted_part = jnp.stack([real, imag])[:, inverse, :]  14.2 us
    select_n x1, other arithmetic, local(): next_wave = jnp.where(last_k, permuted, received)  10.2 us
    unnamed x30, local copies, waits for them, and re-layouts  8.5 us
  transfers between devices with their start and end apart: 4, of which 3 were waited for; matrix products, arithmetic and copies ran while one was open for 29% of the time, Pallas kernels for 0%

commit v1 on v0

v1 whole, which is shorter than its diff:
```python
import functools

import jax
import jax.numpy as jnp
from jax import lax
from jax.experimental import pallas as pl
from jax.experimental.pallas import tpu as pltpu
from jax.sharding import PartitionSpec as P

PPA = 18
MESH = pl.DeviceIdType.MESH


def from_behind(block, axis, distance):
    devices = range(lax.axis_size(axis))
    route = [((i - distance) % len(devices), i) for i in devices]
    return lax.ppermute(block, axis, route)


def contract(left, right, precision=None):
    return lax.dot_general(
        left,
        right,
        (((0,), (0,)), ((), ())),
        precision=precision,
        preferred_element_type=jnp.float32,
    )


def orders_of(n):
    bits = n.bit_length() - 1
    first = list(range(bits))
    second = [0] + list(range(2, bits)) + [1] if bits > 2 else first
    return first, second


def expand(me, done, free, count):
    index = me & sum(1 << bit for bit in done)
    for place, bit in enumerate(free):
        index = index | (((count >> place) & 1) << bit)
    return index


def halving(n, me, acc, sends, recvs, send_scales, recv_scales, sems):
    orders = orders_of(n)
    bits = len(orders[0])
    rows = acc.shape[2]

    def copies(stream, stage):
        size = n >> (stage + 1)
        base = n - (n >> stage)
        bit = orders[stream][stage]
        partner = me ^ (1 << bit)
        made = []
        for kind, (src, dst) in enumerate(((sends, recvs), (send_scales, recv_scales))):
            made.append(
                pltpu.make_async_remote_copy(
                    src_ref=src.at[stream, pl.ds(base, size)],
                    dst_ref=dst.at[stream, pl.ds(base, size)],
                    send_sem=sems.at[0, stream, stage, kind],
                    recv_sem=sems.at[1, stream, stage, kind],
                    device_id={"pw": partner},
                    device_id_type=MESH,
                )
            )
        return made

    def push(stream, stage):
        size = n >> (stage + 1)
        base = n - (n >> stage)
        bit = orders[stream][stage]
        done = orders[stream][:stage]
        free = [b for b in orders[stream][stage + 1 :]]
        partner = me ^ (1 << bit)

        def code(count, carry):
            chunk = expand(partner, done + [bit], free, count)
            x = acc[stream, chunk]
            top = jnp.max(jnp.abs(x), axis=0, keepdims=True)
            scale = jnp.maximum(top, 1e-30) * (1.0 / 32767.0)
            q = jnp.floor(x * (1.0 / scale) + 0.5)
            sends[stream, base + count] = q.astype(jnp.int32).astype(jnp.int16)
            send_scales[stream, base + count] = scale
            return carry

        lax.fori_loop(0, size, code, 0)
        for copy in copies(stream, stage):
            copy.start()

    def pull(stream, stage):
        size = n >> (stage + 1)
        base = n - (n >> stage)
        bit = orders[stream][stage]
        done = orders[stream][:stage]
        free = [b for b in orders[stream][stage + 1 :]]
        for copy in copies(stream, stage):
            copy.wait()

        def add(count, carry):
            chunk = expand(me, done + [bit], free, count)
            q = recvs[stream, base + count].astype(jnp.int32).astype(jnp.float32)
            acc[stream, chunk] = acc[stream, chunk] + q * recv_scales[stream, base + count]
            return carry

        lax.fori_loop(0, size, add, 0)

    return push, pull, bits


def greet(n, me):
    barrier = pltpu.get_barrier_semaphore()
    bits = n.bit_length() - 1
    for bit in range(bits):
        pl.semaphore_signal(barrier, inc=1, device_id={"pw": me ^ (1 << bit)}, device_id_type=MESH)
    pl.semaphore_wait(barrier, bits)


def scatter_scratch(n, rows, cols):
    bits = n.bit_length() - 1
    return [
        pltpu.VMEM((2, n, rows, cols), jnp.float32),
        pltpu.VMEM((2, n, rows, cols), jnp.int16),
        pltpu.VMEM((2, n, rows, cols), jnp.int16),
        pltpu.VMEM((2, n, 1, cols), jnp.float32),
        pltpu.VMEM((2, n, 1, cols), jnp.float32),
        pltpu.SemaphoreType.DMA((2, 2, bits, 2)),
    ]


def sorted_scatter_kernel(n, inverse, real, imag, out, acc, *rest):
    me = lax.axis_index("pw")
    rows = acc.shape[2]
    greet(n, me)
    push, pull, bits = halving(n, me, acc, *rest)

    def gather(owner_bit, count):
        chunk = ((count << 1) | owner_bit)

        def eight(group, carry):
            for r in range(16):
                row = group * 16 + r
                at = inverse[chunk * rows + row]
                acc[0, chunk, pl.ds(row, 1), :] = real[pl.ds(at, 1), :]
                acc[1, chunk, pl.ds(row, 1), :] = imag[pl.ds(at, 1), :]
            return carry

        lax.fori_loop(0, rows // 16, eight, 0)

    lax.fori_loop(0, n // 2, lambda c, k: (gather(1 - (me & 1), c), k)[1], 0)
    for stream in range(2):
        push(stream, 0)
    lax.fori_loop(0, n // 2, lambda c, k: (gather(me & 1, c), k)[1], 0)
    for stage in range(bits):
        for stream in range(2):
            pull(stream, stage)
            if stage + 1 < bits:
                push(stream, stage + 1)
    out[0] = acc[0, me]
    out[1] = acc[1, me]


def plain_scatter_kernel(n, source, out, acc, *rest):
    me = lax.axis_index("pw")
    greet(n, me)
    push, pull, bits = halving(n, me, acc, *rest)

    def fill(count, carry):
        acc[0, count] = source[0, count]
        acc[1, count] = source[1, count]
        return carry

    lax.fori_loop(0, n, fill, 0)
    for stream in range(2):
        push(stream, 0)
    for stage in range(bits):
        for stream in range(2):
            pull(stream, stage)
            if stage + 1 < bits:
                push(stream, stage + 1)
    out[0] = acc[0, me]
    out[1] = acc[1, me]


def vmem():
    return pl.BlockSpec(memory_space=pltpu.VMEM)


def sorted_scatter(n, inverse, real, imag):
    rows, cols = real.shape[0] // n, real.shape[1]
    return pl.pallas_call(
        functools.partial(sorted_scatter_kernel, n),
        out_shape=jax.ShapeDtypeStruct((2, rows, cols), jnp.float32),
        in_specs=[pl.BlockSpec(memory_space=pltpu.SMEM), vmem(), vmem()],
        out_specs=vmem(),
        scratch_shapes=scatter_scratch(n, rows, cols),
        compiler_params=pltpu.CompilerParams(collective_id=0, has_side_effects=True, vmem_limit_bytes=40 * 2**20),
        cost_estimate=pl.CostEstimate(flops=0, bytes_accessed=60 * 10**6, transcendentals=0),
    )(inverse, real, imag)


def plain_scatter(n, source):
    rows, cols = source.shape[2], source.shape[3]
    return pl.pallas_call(
        functools.partial(plain_scatter_kernel, n),
        out_shape=jax.ShapeDtypeStruct((2, rows, cols), jnp.float32),
        in_specs=[vmem()],
        out_specs=vmem(),
        scratch_shapes=scatter_scratch(n, rows, cols),
        compiler_params=pltpu.CompilerParams(collective_id=1, has_side_effects=True, vmem_limit_bytes=20 * 2**20),
    )(source)


def invert(order, size):
    place = lax.broadcasted_iota(jnp.int32, (size, size), 1)
    slot = lax.broadcasted_iota(jnp.int32, (size, size), 0)
    return jnp.sum(jnp.where(order[None, :] == slot, place, 0), axis=1)


def local(waves, projectors, projector_order, shift_map, charges, atom_phase):
    wave = waves[0]
    beta = projectors[0]
    n = lax.axis_size("pw")
    pw_dev, nb = wave.shape[1], wave.shape[2]
    last_k = lax.axis_index("ka") == lax.axis_size("ka") - 1
    pw_index = lax.axis_index("pw")
    received = from_behind(wave, "ka", -1)
    real = contract(beta[0], wave[0]) + contract(beta[1], wave[1])
    imag = contract(beta[0], wave[1]) - contract(beta[1], wave[0])
    inverse = invert(projector_order, projector_order.shape[0])
    block = sorted_scatter(n, inverse, real, imag)
    next_block = from_behind(block, "ka", -1)
    local_map = shift_map - pw_index * pw_dev
    target = jnp.where(last_k, local_map, jnp.arange(pw_dev, dtype=jnp.int32))
    hot = (target[None, :] == jnp.arange(pw_dev, dtype=jnp.int32)[:, None]).astype(jnp.bfloat16)
    own = lax.dot_general(
        hot, wave, (((1,), (1,)), ((), ())), preferred_element_type=jnp.float32
    ).astype(jnp.bfloat16)
    own_r, own_i = own[:, 0], own[:, 1]
    atom_dev = block.shape[1] // PPA
    phase = lax.dynamic_slice_in_dim(atom_phase, pw_index * atom_dev, atom_dev)
    phase = jnp.where(last_k, phase, 0.0)
    repeated = jnp.repeat(phase, PPA)
    cosine = jnp.cos(repeated)[:, None]
    sine = jnp.sin(repeated)[:, None]
    raw = lax.dynamic_slice_in_dim(charges, pw_index * atom_dev, atom_dev, 0)
    sym = 0.5 * (raw + jnp.transpose(raw, (0, 2, 1)))
    eye = jnp.eye(atom_dev, dtype=jnp.float32)
    full = (sym[:, :, None, :] * eye[:, None, :, None]).reshape(atom_dev * PPA, atom_dev * PPA)
    high = lax.Precision.HIGHEST
    turned = jnp.concatenate(
        [next_block[0] * cosine + next_block[1] * sine, next_block[1] * cosine - next_block[0] * sine], axis=1
    )
    weighted = jnp.dot(full, turned, precision=high, preferred_element_type=jnp.float32)
    wr, wi = weighted[:, :nb], weighted[:, nb:]
    out_r = contract(own_r, received[0]) + contract(own_i, received[1])
    out_i = contract(own_r, received[1]) - contract(own_i, received[0])
    out_r = out_r + contract(block[0], wr, high) + contract(block[1], wi, high)
    out_i = out_i + contract(block[0], wi, high) - contract(block[1], wr, high)
    source = jnp.stack([out_r.reshape(n, nb // n, nb), out_i.reshape(n, nb // n, nb)])
    summed = plain_scatter(n, source)
    return jnp.transpose(summed, (1, 0, 2))[None]


def solution(mesh):
    placed = (P("ka", None, "pw", None), P("ka", None, "pw", None), P(), P("pw"), P(), P())
    return jax.shard_map(
        local, mesh=mesh, in_specs=placed, out_specs=P("ka", "pw", None, None), check_vma=False
    )
```

time: 301 us -> 138 us (0.46)
  waiting for transfers between devices: 178 us -> 37.6 us
  local copies, waits for them, and re-layouts: 61.4 us -> 5.27 us
  Pallas kernels: 0 us -> 54.1 us
  between operations: 15.1 us -> 0.24 us
  other arithmetic: 16.7 us -> 2.64 us
  matrix products: 24.4 us -> 35.2 us
    unnamed x4 -> x0, waiting for transfers between devices: 175 us -> none
    pallas_call x0 -> x2, Pallas kernels: none -> 54.1 us  [the longest x1 41.8 us: sorted_scatter(): pl.pallas_call(functools.partial(sorted_scatter_kernel, n), out_shape=jax...]
    ppermute x2, waiting for transfers between devices: 2.97 us -> 37.6 us  [from_behind(): return lax.ppermute(block, axis, route)]
    gather x2 -> x0, local copies, waits for them, and re-layouts: 30.9 us -> none  [the longest x1 16.7 us: local(): permuted = jnp.take(received, local_map, axis=1)]
    another operation x1 -> x0, local copies, waits for them, and re-layouts: 14.4 us -> none  [local(): sorted_part = jnp.stack([real, imag])[:, inverse, :]]
    select_n x3 -> x1, other arithmetic: 10.2 us -> 0.01 us  [local(): target = jnp.where(last_k, local_map, jnp.arange(pw_dev, dtype=jnp.int32))]
    dot_general x1 -> x2, matrix products: 0.48 us -> 7.66 us  [the longest x1 7.25 us: local(): lax.dot_general(hot, wave, (((1,), (1,)), ((), ())), preferred_element_ty...]
    sort x1 -> x0, other arithmetic: 5.76 us -> none  [local(): inverse = jnp.argsort(projector_order)]
  transfers between devices with their start and end apart: 4 -> 2, of which waited for: 3 -> 1; matrix products, arithmetic and copies ran while one was open for 29% -> 7% of each run, Pallas kernels for 0% -> 0%
where the time goes in v1:
time: 138 us; the launch traced here: 137 us
  Pallas kernels  54.1 us (39%)
  waiting for transfers between devices  37.6 us (27%)
  matrix products  35.2 us (26%)
  local copies, waits for them, and re-layouts  5.27 us (4%)
  other arithmetic  2.64 us (2%)
  starting transfers between devices  2.09 us (2%)
    pallas_call x1, Pallas kernels, sorted_scatter(): pl.pallas_call(functools.partial(sorted_scatter_kernel, n), out_shape=jax...  41.8 us
    ppermute x2, waiting for transfers between devices, from_behind(): return lax.ppermute(block, axis, route)  37.6 us
    dot_general x12, matrix products, contract(): lax.dot_general(left, right, (((0,), (0,)), ((), ())), precision=precisio...  27.5 us
    pallas_call x1, Pallas kernels, plain_scatter(): pl.pallas_call(functools.partial(plain_scatter_kernel, n), out_shape=jax....  12.3 us
    dot_general x1, matrix products, local(): lax.dot_general(hot, wave, (((1,), (1,)), ((), ())), preferred_element_ty...  7.25 us
    unnamed x12, local copies, waits for them, and re-layouts  3.81 us
  transfers between devices with their start and end apart: 2, of which 1 were waited for; matrix products, arithmetic and copies ran while one was open for 7% of the time, Pallas kernels for 0%

profile of v1, /device:TPU:0, one launch (start us, length us, event | category | flops | bytes accessed | tf_op | source)
XLA Modules:
  0.0 137.2 jit_solution(9564727113292570146)
XLA Ops:
  0.0 5.7 %fusion.5 = f32[2304,256]{1,0:T(8,128)S(1)} fusion(bf16[1,2,2048,2304]{3,2,1,0:T(8,128)(2,1)} %param.7, bf16[1,2,2048,256]{3,2,1,0:T(8,128)(2,1)} %param.6), kind=kOutput, calls=%fused_computation.7 | convolution fusion | flops 2415919104 | bytes 12845056 | tf_op jit(solution)/shard_map/dot_general | solution.py:21
  5.7 3.8 %copy-done.3 = bf16[1,2,2048,2304]{3,2,1,0:T(8,128)(2,1)S(1)} copy-done((bf16[1,2,2048,2304]{3,2,1,0:T(8,128)(2,1)S(1)}, bf16[1,2,2048,2304]{3,2,1,0:T(8,128)(2,1)}, u32[]{:S(2)}) %copy-start.3) | copy-done | bytes 18874392
  9.5 4.1 %fusion.3 = f32[2304,256]{1,0:T(8,128)S(1)} fusion(bf16[1,2,2048,2304]{3,2,1,0:T(8,128)(2,1)S(1)} %copy-done.3, bf16[1,2,2048,256]{3,2,1,0:T(8,128)(2,1)} %param.6), kind=kOutput, calls=%fused_computation.5 | convolution fusion | flops 2415919104 | bytes 12845056 | tf_op jit(solution)/shard_map/dot_general | solution.py:21
  13.6 4.1 %fusion.16.real = f32[2304,256]{1,0:T(8,128)S(1)} fusion(f32[2304,256]{1,0:T(8,128)S(1)} %fusion.5, bf16[1,2,2048,2304]{3,2,1,0:T(8,128)(2,1)S(1)} %copy-done.3, bf16[1,2,2048,256]{3,2,1,0:T(8,128)(2,1)} %param.6), kind=kOutput, calls=%fused_computation.18 | convolution fusion | flops 2416508928 | bytes 15204352 | tf_op jit(solution)/shard_map/dot_general | solution.py:21
  17.7 4.2 %fusion.19.imag = f32[2304,256]{1,0:T(8,128)S(1)} fusion(f32[2304,256]{1,0:T(8,128)S(1)} %fusion.3, bf16[1,2,2048,2304]{3,2,1,0:T(8,128)(2,1)S(1)} %copy-done.3, bf16[1,2,2048,256]{3,2,1,0:T(8,128)(2,1)} %param.6), kind=kOutput, calls=%fused_computation.19 | convolution fusion | flops 2416508928 | bytes 15204352 | tf_op jit(solution)/shard_map/dot_general | solution.py:21
  21.9 2.2 %select_reduce_fusion.inverse = s32[2304]{0:T(1024)S(1)} fusion(s32[2304]{0:T(1024)S(1)} %copy-done.4), kind=kLoop, calls=%fused_computation | loop fusion | flops 15922944 | bytes 18432 | tf_op jit(solution)/shard_map/reduce_sum | solution.py:216
  24.1 41.8 %shard_map.64 = f32[2,144,256]{2,1,0:T(8,128)S(1)} custom-call(s32[2304]{0:T(1024)S(1)} %select_reduce_fusion.inverse, f32[2304,256]{1,0:T(8,128)S(1)} %fusion.16.real, f32[2304,256]{1,0:T(8,128)S(1)} %fusion.19.imag), custom_call_target="tpu_custom_call" | custom-call | bytes 60000000 | tf_op jit(solution)/shard_map/pallas_call | solution.py:190
  65.9 1.6 %collective-permute-start.1 = (f32[2,144,256]{2,1,0:T(8,128)S(1)}, f32[2,144,256]{2,1,0:T(8,128)S(1)}, u32[]{:S(2)}, u32[]{:S(2)}) collective-permute-start(f32[2,144,256]{2,1,0:T(8,128)S(1)} %shard_map.64), channel_id=1, source_target_pairs={{1,0},{0,1},{3,2},{2,3},{5,4},{4,5},{7,6},{6,7},{9,8},{8,9},{11,10... | collective-permute-start | bytes 884744 | tf_op jit(solution)/shard_map/ppermute | solution.py:17
  67.5 0.5 collective-permute-start
  68.3 7.3 %fusion.22 = bf16[2048,2,256]{2,0,1:T(8,128)(2,1)} fusion(s32[2048]{0:T(1024)S(1)} %iota_select_fusion, bf16[1,2,2048,256]{3,2,1,0:T(8,128)(2,1)} %param.6), kind=kOutput, calls=%fused_computation.20 | convolution fusion | flops 4300210176 | bytes 4202496 | tf_op jit(solution)/shard_map/dot_general | solution.py:235
  75.9 0.2 copy.11
  76.3 0.2 mul.65
  76.6 0.4 fusion.37
  77.0 0.7 fusion.46
  77.7 0.7 fusion.44
  78.3 37.6 %collective-permute-done = bf16[2,2048,256]{2,1,0:T(8,128)(2,1)} collective-permute-done((bf16[2,2048,256]{2,1,0:T(8,128)(2,1)}, bf16[2,2048,256]{2,1,0:T(8,128)(2,1)}, u32[]{:S(2)}, u32[]{:S(2)}) %collective-permute-start) | collective-permute-done | bytes 2097184 | tf_op jit(solution)/shard_map/ppermute | solution.py:17
  116.0 1.7 %fusion.32 = f32[256,256]{1,0:T(8,128)S(1)} fusion(bf16[2048,2,256]{2,0,1:T(8,128)(2,1)S(1)} %copy-done.5, bf16[2,2048,256]{2,1,0:T(8,128)(2,1)} %collective-permute-done), kind=kOutput, calls=%fused_computation.36 | convolution fusion | flops 268435456 | bytes 2359296 | tf_op jit(solution)/shard_map/dot_general | solution.py:21
  117.7 1.7 %fusion.26 = f32[256,256]{1,0:T(8,128)S(1)} fusion(f32[256,256]{1,0:T(8,128)S(1)} %fusion.46, f32[256,256]{1,0:T(8,128)S(1)} %fusion.32, bf16[2048,2,256]{2,0,1:T(8,128)(2,1)S(1)} %copy-done.5, bf16[2,2048,256]{2,1,0:T(8,128)(2,1)} %collective-permute-done), kind=kOutput, calls=%fused_computation.26 | convolution fusion | flops 268566528 | bytes 2883584 | tf_op jit(solution)/shard_map/dot_general | solution.py:21
  119.4 0.7 convolution_add_fusion
  120.1 1.7 %fusion.31 = f32[256,256]{1,0:T(8,128)S(1)} fusion(bf16[2,2048,256]{2,1,0:T(8,128)(2,1)} %collective-permute-done, bf16[2048,2,256]{2,0,1:T(8,128)(2,1)S(1)} %copy-done.5), kind=kOutput, calls=%fused_computation.35 | convolution fusion | flops 268435456 | bytes 2359296 | tf_op jit(solution)/shard_map/dot_general | solution.py:21
  121.8 1.7 %fusion.25 = f32[256,256]{1,0:T(8,128)S(1)} fusion(f32[256,256]{1,0:T(8,128)S(1)} %fusion.44, f32[256,256]{1,0:T(8,128)S(1)} %fusion.31, bf16[2048,2,256]{2,0,1:T(8,128)(2,1)S(1)} %copy-done.5, bf16[2,2048,256]{2,1,0:T(8,128)(2,1)} %collective-permute-done), kind=kOutput, calls=%fused_computation.24 | convolution fusion | flops 268566528 | bytes 2883584 | tf_op jit(solution)/shard_map/dot_general | solution.py:21
  123.5 0.7 convolution_subtract_fusion
  124.2 12.3 %shard_map.65 = f32[2,16,256]{2,1,0:T(8,128)S(1)} custom-call(f32[2,16,16,256]{3,2,1,0:T(8,128)S(1)} %pad_maximum_fusion.source), custom_call_target="tpu_custom_call" | custom-call | tf_op jit(solution)/shard_map/pallas_call | solution.py:203
  136.6 0.6 copy.12
  (24 shorter events, 0.9 us)
Async XLA Ops:
  0.0 68.0 %copy-start = (f32[128,18,18]{0,2,1:T(8,128)S(1)}, f32[128,18,18]{0,2,1:T(8,128)}, u32[]{:S(2)}) copy-start(f32[128,18,18]{0,2,1:T(8,128)} %param.10) | copy-start | bytes 497668
  0.0 9.5 %copy-start.3 = (bf16[1,2,2048,2304]{3,2,1,0:T(8,128)(2,1)S(1)}, bf16[1,2,2048,2304]{3,2,1,0:T(8,128)(2,1)}, u32[]{:S(2)}) copy-start(bf16[1,2,2048,2304]{3,2,1,0:T(8,128)(2,1)} %param.7) | copy-start | bytes 56623108
  17.7 4.2 %copy-start.4 = (s32[2304]{0:T(1024)S(1)}, s32[2304]{0:T(1024)}, u32[]{:S(2)}) copy-start(s32[2304]{0:T(1024)} %param.8) | copy-start | bytes 27652
  24.1 44.1 %copy-start.1 = (s32[2048]{0:T(1024)S(1)}, s32[2048]{0:T(1024)}, u32[]{:S(2)}) copy-start(s32[2048]{0:T(1024)} %param.9) | copy-start | bytes 24580
  65.9 10.5 %collective-permute-start.1 = (f32[2,144,256]{2,1,0:T(8,128)S(1)}, f32[2,144,256]{2,1,0:T(8,128)S(1)}, u32[]{:S(2)}, u32[]{:S(2)}) collective-permute-start(f32[2,144,256]{2,1,0:T(8,128)S(1)} %shard_map.64), channel_id=1, source_target_pairs={{1,0},{0,1},{3,2},{2,3},{5,4},{4,5},{7,6},{6,7},{9,8},{8,9},{11,10... | collective-permute-start | bytes 884744 | tf_op jit(solution)/shard_map/ppermute | solution.py:17
  67.5 48.5 %collective-permute-start = (bf16[2,2048,256]{2,1,0:T(8,128)(2,1)}, bf16[2,2048,256]{2,1,0:T(8,128)(2,1)}, u32[]{:S(2)}, u32[]{:S(2)}) collective-permute-start(bf16[2,2048,256]{2,1,0:T(8,128)(2,1)} %bitcast.1), channel_id=1, source_target_pairs={{1,0},{0,1},{3,2},{2,3},{5,4},{4,5},{7,6},{6,7},{9,8},{8,9},{11,10... | collective-permute-start | bytes 6291464 | tf_op jit(solution)/shard_map/ppermute | solution.py:17
  68.2 7.3 %copy-start.2 = (f32[128]{0:T(128)S(1)}, f32[128]{0:T(128)}, u32[]{:S(2)}) copy-start(f32[128]{0:T(128)} %param.11) | copy-start | bytes 1540
  76.5 39.5 %copy-start.5 = (bf16[2048,2,256]{2,0,1:T(8,128)(2,1)S(1)}, bf16[2048,2,256]{2,0,1:T(8,128)(2,1)}, u32[]{:S(2)}) copy-start(bf16[2048,2,256]{2,0,1:T(8,128)(2,1)} %fusion.22) | copy-start | bytes 6291460

commit v2 on v1

v2 whole, which is shorter than its diff:
```python
import functools

import jax
import jax.numpy as jnp
from jax import lax
from jax.experimental import pallas as pl
from jax.experimental.pallas import tpu as pltpu
from jax.sharding import PartitionSpec as P

PPA = 18
MESH = pl.DeviceIdType.MESH


def contract(left, right, precision=None):
    return lax.dot_general(
        left,
        right,
        (((0,), (0,)), ((), ())),
        precision=precision,
        preferred_element_type=jnp.float32,
    )


def orders_of(n):
    bits = n.bit_length() - 1
    first = list(range(bits))
    second = [0] + list(range(2, bits)) + [1] if bits > 2 else first
    return first, second


def expand(me, done, free, count):
    index = me & sum(1 << bit for bit in done)
    for place, bit in enumerate(free):
        index = index | (((count >> place) & 1) << bit)
    return index


def halving(n, me, acc, sends, recvs, send_scales, recv_scales, sems):
    orders = orders_of(n)
    bits = len(orders[0])
    rows = acc.shape[2]

    def copies(stream, stage):
        size = n >> (stage + 1)
        base = n - (n >> stage)
        bit = orders[stream][stage]
        partner = me ^ (1 << bit)
        made = []
        for kind, (src, dst) in enumerate(((sends, recvs), (send_scales, recv_scales))):
            made.append(
                pltpu.make_async_remote_copy(
                    src_ref=src.at[stream, pl.ds(base, size)],
                    dst_ref=dst.at[stream, pl.ds(base, size)],
                    send_sem=sems.at[0, stream, stage, kind],
                    recv_sem=sems.at[1, stream, stage, kind],
                    device_id={"pw": partner},
                    device_id_type=MESH,
                )
            )
        return made

    def push(stream, stage):
        size = n >> (stage + 1)
        base = n - (n >> stage)
        bit = orders[stream][stage]
        done = orders[stream][:stage]
        free = [b for b in orders[stream][stage + 1 :]]
        partner = me ^ (1 << bit)

        def code(count, carry):
            chunk = expand(partner, done + [bit], free, count)
            x = acc[stream, chunk]
            top = jnp.max(jnp.abs(x), axis=0, keepdims=True)
            scale = jnp.maximum(top, 1e-30) * (1.0 / 32767.0)
            q = jnp.floor(x * (1.0 / scale) + 0.5)
            sends[stream, base + count] = q.astype(jnp.int32).astype(jnp.int16)
            send_scales[stream, base + count] = scale
            return carry

        lax.fori_loop(0, size, code, 0)
        for copy in copies(stream, stage):
            copy.start()

    def pull(stream, stage):
        size = n >> (stage + 1)
        base = n - (n >> stage)
        bit = orders[stream][stage]
        done = orders[stream][:stage]
        free = [b for b in orders[stream][stage + 1 :]]
        for copy in copies(stream, stage):
            copy.wait()

        def add(count, carry):
            chunk = expand(me, done + [bit], free, count)
            q = recvs[stream, base + count].astype(jnp.int32).astype(jnp.float32)
            acc[stream, chunk] = acc[stream, chunk] + q * recv_scales[stream, base + count]
            return carry

        lax.fori_loop(0, size, add, 0)

    return push, pull, bits


def fused_kernel(
    n, kn, inverse, target, cosine, sine, sym, wave_hbm, beta_hbm, out,
    wave, beta, rhs, proj, received, own, mine, nextb, kept, local_sems, ka_sems, *scratch
):
    me = lax.axis_index("pw")
    k = lax.axis_index("ka")
    ahead, behind = lax.rem(k + 1, kn), lax.rem(k + kn - 1, kn)
    acc, first = scratch[0], scratch[:6]
    last = scratch[6:]
    acc_last = last[0]
    pw_dev, nb = wave.shape[1], wave.shape[2]
    half = nb // 2
    rows = acc.shape[2]
    tiles = local_sems.shape[0] - 1
    tile = beta.shape[2] // tiles

    def beta_copy(t):
        at = pl.ds(pl.multiple_of(t * tile, tile), tile)
        return pltpu.make_async_copy(beta_hbm.at[0, :, :, at], beta.at[:, :, at], local_sems.at[t + 1])

    own_copy = pltpu.make_async_copy(wave_hbm.at[0], wave, local_sems.at[0])
    own_copy.start()
    for t in range(tiles):
        beta_copy(t).start()

    barrier = pltpu.get_barrier_semaphore()
    bits = n.bit_length() - 1
    for bit in range(bits):
        pl.semaphore_signal(barrier, inc=1, device_id={"pw": me ^ (1 << bit)}, device_id_type=MESH)
    for other in (ahead, behind):
        pl.semaphore_signal(barrier, inc=1, device_id={"ka": other}, device_id_type=MESH)
    pl.semaphore_wait(barrier, bits + 2)

    def ka_copy(src, dst, at):
        return pltpu.make_async_remote_copy(
            src_ref=src,
            dst_ref=dst,
            send_sem=ka_sems.at[0, at],
            recv_sem=ka_sems.at[1, at],
            device_id={"ka": behind},
            device_id_type=MESH,
        )

    wave_copy = ka_copy(wave_hbm.at[0], received, 0)
    wave_copy.start()
    own_copy.wait()
    for stream in range(2):
        cols = slice(stream * half, (stream + 1) * half)
        rhs[stream, 0, :, :half] = wave[0, :, cols]
        rhs[stream, 0, :, half:] = wave[1, :, cols]
        rhs[stream, 1, :, :half] = wave[1, :, cols]
        rhs[stream, 1, :, half:] = -wave[0, :, cols]

    push, pull, bits = halving(n, me, *first)

    def multiply(stream, low, high):
        def step(t, carry):
            if stream == 0:
                beta_copy(t).wait()
            at = pl.ds(pl.multiple_of(t * tile, tile), tile)
            proj[stream, at, :] = contract(beta[0, :, at], rhs[stream, 0]) + contract(beta[1, :, at], rhs[stream, 1])
            return carry

        lax.fori_loop(low, high, step, 0)

    def gather(stream, core):
        def one(count, carry):
            chunk = (count << 1) | core

            def some(group, inner):
                for r in range(16):
                    row = group * 16 + r
                    at = inverse[chunk * rows + row]
                    acc[stream, chunk, pl.ds(row, 1), :] = proj[stream, pl.ds(at, 1), :]
                return inner

            lax.fori_loop(0, rows // 16, some, 0)
            return carry

        lax.fori_loop(0, n // 2, one, 0)

    def permute_own(low, high):
        block = 256 if pw_dev % 256 == 0 else pw_dev

        def step(b, carry):
            at = pl.ds(pl.multiple_of(b * block, block), block)
            slot = lax.broadcasted_iota(jnp.int32, (block, pw_dev), 0) + b * block
            hot = jnp.where(slot == target[...], 1.0, 0.0).astype(jnp.bfloat16)
            for part in range(2):
                own[part, at, :] = jnp.dot(hot, wave[part], preferred_element_type=jnp.float32).astype(jnp.bfloat16)
            return carry

        lax.fori_loop(low * (pw_dev // block) // 2, high * (pw_dev // block) // 2, step, 0)

    multiply(0, 0, tiles)
    gather(0, 1 - (me & 1))
    push(0, 0)
    gather(0, me & 1)
    multiply(1, 0, (tiles + 1) // 2)
    pull(0, 0)
    push(0, 1)
    multiply(1, (tiles + 1) // 2, tiles)
    gather(1, 1 - (me & 1))
    push(1, 0)
    gather(1, me & 1)
    permute_own(0, 1)
    pull(0, 1)
    push(0, 2)
    pull(1, 0)
    push(1, 1)
    permute_own(1, 2)

    def finish(stream):
        mine[stream] = acc[stream, me]
        ka_copy(mine.at[stream], nextb.at[stream], 1 + stream).start()

    for stage in range(2, bits):
        pull(0, stage)
        if stage + 1 < bits:
            push(0, stage + 1)
        else:
            finish(0)
        pull(1, stage - 1)
        push(1, stage)
    wave_copy.wait()
    def plane():
        a, b = received[0], received[1]
        c, d = own[0], own[1]
        kept[0] = contract(c, a) + contract(d, b)
        kept[1] = contract(c, b) - contract(d, a)
    plane()
    pull(1, bits - 1)
    finish(1)
    for stream in range(2):
        ka_copy(mine.at[stream], nextb.at[stream], 1 + stream).wait()
    high = lax.Precision.HIGHEST
    nr = jnp.concatenate([nextb[0, :, :half], nextb[1, :, :half]], axis=1)
    ni = jnp.concatenate([nextb[0, :, half:], nextb[1, :, half:]], axis=1)
    br = jnp.concatenate([mine[0, :, :half], mine[1, :, :half]], axis=1)
    bi = jnp.concatenate([mine[0, :, half:], mine[1, :, half:]], axis=1)
    cos, sin = cosine[...], sine[...]
    charge = sym[...]
    wr = jnp.dot(charge, nr * cos + ni * sin, precision=high, preferred_element_type=jnp.float32)
    wi = jnp.dot(charge, ni * cos - nr * sin, precision=high, preferred_element_type=jnp.float32)
    kept[0] += contract(br, wr, high) + contract(bi, wi, high)
    kept[1] += contract(br, wi, high) - contract(bi, wr, high)
    share = nb // n

    def fill(count, carry):
        at = pl.ds(pl.multiple_of(count * share, share), share)
        acc_last[0, count] = kept[0, at, :]
        acc_last[1, count] = kept[1, at, :]
        return carry

    lax.fori_loop(0, n, fill, 0)
    push, pull, bits = halving(n, me, *last)
    for stream in range(2):
        push(stream, 0)
    for stage in range(bits):
        for stream in range(2):
            pull(stream, stage)
            if stage + 1 < bits:
                push(stream, stage + 1)
    out[0] = acc_last[0, me]
    out[1] = acc_last[1, me]


def scatter_scratch(n, rows, cols):
    bits = n.bit_length() - 1
    return [
        pltpu.VMEM((2, n, rows, cols), jnp.float32),
        pltpu.VMEM((2, n, rows, cols), jnp.int16),
        pltpu.VMEM((2, n, rows, cols), jnp.int16),
        pltpu.VMEM((2, n, 1, cols), jnp.float32),
        pltpu.VMEM((2, n, 1, cols), jnp.float32),
        pltpu.SemaphoreType.DMA((2, 2, bits, 2)),
    ]


def vmem():
    return pl.BlockSpec(memory_space=pltpu.VMEM)


def fused(n, kn, inverse, target, cosine, sine, sym, waves, projectors):
    pw_dev, nb = waves.shape[2], waves.shape[3]
    nproj = projectors.shape[3]
    rows, share = nproj // n, nb // n
    tile = 256 if nproj % 256 == 0 else 128 if nproj % 128 == 0 else nproj
    hbm = pl.BlockSpec(memory_space=pl.ANY)
    return pl.pallas_call(
        functools.partial(fused_kernel, n, kn),
        out_shape=jax.ShapeDtypeStruct((2, share, nb), jnp.float32),
        in_specs=[pl.BlockSpec(memory_space=pltpu.SMEM), vmem(), vmem(), vmem(), vmem(), hbm, hbm],
        out_specs=vmem(),
        scratch_shapes=[
            pltpu.VMEM((2, pw_dev, nb), jnp.bfloat16),
            pltpu.VMEM((2, pw_dev, nproj), jnp.bfloat16),
            pltpu.VMEM((2, 2, pw_dev, nb), jnp.bfloat16),
            pltpu.VMEM((2, nproj, nb), jnp.float32),
            pltpu.VMEM((2, pw_dev, nb), jnp.bfloat16),
            pltpu.VMEM((2, pw_dev, nb), jnp.bfloat16),
            pltpu.VMEM((2, rows, nb), jnp.float32),
            pltpu.VMEM((2, rows, nb), jnp.float32),
            pltpu.VMEM((2, nb, nb), jnp.float32),
            pltpu.SemaphoreType.DMA((nproj // tile + 1,)),
            pltpu.SemaphoreType.DMA((2, 3)),
        ]
        + scatter_scratch(n, rows, nb)
        + scatter_scratch(n, share, nb),
        compiler_params=pltpu.CompilerParams(
            collective_id=0, has_side_effects=True, vmem_limit_bytes=62 * 2**20
        ),
    )(inverse, target, cosine, sine, sym, waves, projectors)


def invert(order, size):
    place = lax.broadcasted_iota(jnp.int32, (size, size), 1)
    slot = lax.broadcasted_iota(jnp.int32, (size, size), 0)
    return jnp.sum(jnp.where(order[None, :] == slot, place, 0), axis=1)


def local(waves, projectors, projector_order, shift_map, charges, atom_phase):
    n = lax.axis_size("pw")
    kn = lax.axis_size("ka")
    pw_dev = waves.shape[2]
    last_k = lax.axis_index("ka") == kn - 1
    pw_index = lax.axis_index("pw")
    inverse = invert(projector_order, projector_order.shape[0])
    local_map = shift_map - pw_index * pw_dev
    target = jnp.where(last_k, local_map, jnp.arange(pw_dev, dtype=jnp.int32))[None, :]
    atom_dev = atom_phase.shape[0] // n
    phase = lax.dynamic_slice_in_dim(atom_phase, pw_index * atom_dev, atom_dev)
    phase = jnp.where(last_k, phase, 0.0)
    repeated = jnp.repeat(phase, PPA)
    cosine = jnp.cos(repeated)[:, None]
    sine = jnp.sin(repeated)[:, None]
    raw = lax.dynamic_slice_in_dim(charges, pw_index * atom_dev, atom_dev, 0)
    sym = 0.5 * (raw + jnp.transpose(raw, (0, 2, 1)))
    eye = jnp.eye(atom_dev, dtype=jnp.float32)
    full = (sym[:, :, None, :] * eye[:, None, :, None]).reshape(atom_dev * PPA, atom_dev * PPA)
    summed = fused(n, kn, inverse, target, cosine, sine, full, waves, projectors)
    return jnp.transpose(summed, (1, 0, 2))[None]


def solution(mesh):
    placed = (P("ka", None, "pw", None), P("ka", None, "pw", None), P(), P("pw"), P(), P())
    return jax.shard_map(
        local, mesh=mesh, in_specs=placed, out_specs=P("ka", "pw", None, None), check_vma=False
    )
```

time: 138 us -> 95 us (0.69)
  waiting for transfers between devices: 37.6 us -> 0 us
  matrix products: 35.2 us -> 0 us
  Pallas kernels: 54.1 us -> 84.8 us
  other arithmetic: 2.64 us -> 5.77 us
  starting transfers between devices: 2.09 us -> 0 us
    ppermute x2 -> x0, waiting for transfers between devices: 37.6 us -> none  [from_behind(): return lax.ppermute(block, axis, route)]
    dot_general x14 -> x0, matrix products: 35.2 us -> none  [the longest x12 27.5 us: contract(): lax.dot_general(left, right, (((0,), (0,)), ((), ())), precision=precisio...]
    pallas_call x2 -> x1, Pallas kernels: 54.1 us -> 84.8 us  [fused(): pl.pallas_call(functools.partial(fused_kernel, n, kn), out_shape=jax.Shap...]
    unnamed x12 -> x2, local copies, waits for them, and re-layouts: 3.81 us -> 0.01 us
    ppermute x2 -> x0, starting transfers between devices: 2.09 us -> none  [from_behind(): return lax.ppermute(block, axis, route)]
  transfers between devices with their start and end apart: 2 -> 0, of which waited for: 1 -> 0; matrix products, arithmetic and copies ran while one was open for 7% -> 0% of each run, Pallas kernels for 0% -> 0%
where the time goes in v2:
time: 95 us; the launch traced here: 94.7 us
  Pallas kernels  84.8 us (89%)
  other arithmetic  5.77 us (6%)
  local copies, waits for them, and re-layouts  4.14 us (4%)
    pallas_call x1, Pallas kernels, fused(): pl.pallas_call(functools.partial(fused_kernel, n, kn), out_shape=jax.Shap...  84.8 us
    reduce_sum x1, other arithmetic, invert(): return jnp.sum(jnp.where(order[None, :] == slot, place, 0), axis=1)  3.5 us

profile of v2, /device:TPU:0, one launch (start us, length us, event | category | flops | bytes accessed | tf_op | source)
XLA Modules:
  0.0 94.7 jit_solution(12566642003997192733)
XLA Ops:
  0.0 0.0 copy-start
  0.0 0.8 fusion.2
  0.8 0.1 broadcast_in_dim.27
  0.9 0.7 cos.16.cosine
  1.6 0.1 broadcast_in_dim.28
  1.7 0.7 sin.16.sine
  2.4 0.0 copy-done
  2.4 0.1 constant_dynamic-slice_fusion
  2.5 0.1 fusion
  2.6 0.2 copy.16
  2.8 0.1 broadcast_multiply_fusion
  2.9 0.9 mul.37.sym
  3.7 1.3 %iota_select_fusion = s32[2048]{0:T(1024)} fusion(s32[2048]{0:T(1024)} %param.9, s32[]{:T(128)S(6)} %mul.30, pred[]{:T(512)S(6)} %eq.20), kind=kLoop, calls=%fused_computation.5 | loop fusion | flops 4096 | bytes 16389 | tf_op jit(solution)/shard_map/jit(_where)/select_n | solution.py:333
  5.0 3.5 %select_reduce_fusion.inverse = s32[2304]{0:T(1024)} fusion(s32[2304]{0:T(1024)} %param.8), kind=kLoop, calls=%fused_computation | loop fusion | flops 15922944 | bytes 18432 | tf_op jit(solution)/shard_map/reduce_sum | solution.py:322
  8.5 84.8 %shard_map.64 = f32[2,16,256]{2,1,0:T(8,128)} custom-call(s32[2304]{0:T(1024)} %select_reduce_fusion.inverse, s32[1,2048]{1,0:T(1,128)} %bitcast.11, f32[144,1]{1,0:T(8,128)} %cos.16.cosine, f32[144,1]{1,0:T(8,128)} %sin.16.sine, f32[144,144]{1,0:T(8,128)} %mul.37.sym, bf16[1,2,2048,256]{3,2,1,0:T(8,128)(2,1)} %wave_hbm.1, bf16[1,2,2048,2304]{3,2,1,0:T(8,128)(2,1)} %beta_hbm.1), custom_call_target="tpu_custom_call" | custom-call | tf_op jit(solution)/shard_map/pallas_call | solution.py:293
  93.3 1.4 %copy.19 = f32[1,16,2,256]{3,2,1,0:T(2,128)} copy(f32[1,16,2,256]{3,1,2,0:T(8,128)} %bitcast.10) | data formatting | bytes 65536 | tf_op jit(solution)/shard_map/broadcast_in_dim | solution.py:345
  (1 shorter events, 0.0 us)
Async XLA Ops:
  0.0 2.4 %copy-start = (f32[128,18,18]{0,2,1:T(8,128)S(1)}, f32[128,18,18]{0,2,1:T(8,128)}, u32[]{:S(2)}) copy-start(f32[128,18,18]{0,2,1:T(8,128)} %param.10) | copy-start | bytes 497668

commit v3 on v2

--- a/solution.py
+++ b/solution.py
@@ -35,8 +35,7 @@
     return index
 
 
-def halving(n, me, acc, sends, recvs, send_scales, recv_scales, sems):
-    orders = orders_of(n)
+def halving(n, me, orders, acc, sends, recvs, send_scales, recv_scales, sems):
     bits = len(orders[0])
     rows = acc.shape[2]
 
@@ -102,7 +101,7 @@
 
 
 def fused_kernel(
-    n, kn, inverse, target, cosine, sine, sym, wave_hbm, beta_hbm, out,
+    n, kn, inverse, shift, cosine, sine, sym, wave_hbm, beta_hbm, out,
     wave, beta, rhs, proj, received, own, mine, nextb, kept, local_sems, ka_sems, *scratch
 ):
     me = lax.axis_index("pw")
@@ -154,7 +153,7 @@
         rhs[stream, 1, :, :half] = wave[1, :, cols]
         rhs[stream, 1, :, half:] = -wave[0, :, cols]
 
-    push, pull, bits = halving(n, me, *first)
+    push, pull, bits = halving(n, me, (orders_of(n)[0],) * 2, *first)
 
     def multiply(stream, low, high):
         def step(t, carry):
@@ -166,21 +165,26 @@
 
         lax.fori_loop(low, high, step, 0)
 
+    unit = 48 if rows % 48 == 0 else 16 if rows % 16 == 0 else 1
+
     def gather(stream, core):
         def one(count, carry):
             chunk = (count << 1) | core
 
             def some(group, inner):
-                for r in range(16):
-                    row = group * 16 + r
-                    at = inverse[chunk * rows + row]
-                    acc[stream, chunk, pl.ds(row, 1), :] = proj[stream, pl.ds(at, 1), :]
+                low = pl.multiple_of(group * unit, unit)
+                ats = [inverse[chunk * rows + low + r] for r in range(unit)]
+                taken = [proj[stream, pl.ds(at, 1), :] for at in ats]
+                acc[stream, chunk, pl.ds(low, unit), :] = jnp.concatenate(taken, axis=0)
                 return inner
 
-            lax.fori_loop(0, rows // 16, some, 0)
+            lax.fori_loop(0, rows // unit, some, 0)
             return carry
 
         lax.fori_loop(0, n // 2, one, 0)
+
+    every = lax.broadcasted_iota(jnp.int32, (1, pw_dev), 1)
+    target = jnp.where(k == kn - 1, shift[...] - me * pw_dev, every)
 
     def permute_own(low, high):
         block = 256 if pw_dev % 256 == 0 else pw_dev
@@ -188,43 +192,44 @@
         def step(b, carry):
             at = pl.ds(pl.multiple_of(b * block, block), block)
             slot = lax.broadcasted_iota(jnp.int32, (block, pw_dev), 0) + b * block
-            hot = jnp.where(slot == target[...], 1.0, 0.0).astype(jnp.bfloat16)
+            hot = jnp.where(slot == target, 1.0, 0.0).astype(jnp.bfloat16)
             for part in range(2):
                 own[part, at, :] = jnp.dot(hot, wave[part], preferred_element_type=jnp.float32).astype(jnp.bfloat16)
             return carry
 
         lax.fori_loop(low * (pw_dev // block) // 2, high * (pw_dev // block) // 2, step, 0)
+
+    def finish(stream):
+        mine[stream] = acc[stream, me]
+        ka_copy(mine.at[stream], nextb.at[stream], 1 + stream).start()
 
     multiply(0, 0, tiles)
     gather(0, 1 - (me & 1))
     push(0, 0)
     gather(0, me & 1)
-    multiply(1, 0, (tiles + 1) // 2)
+    multiply(1, 0, 1)
     pull(0, 0)
     push(0, 1)
-    multiply(1, (tiles + 1) // 2, tiles)
+    multiply(1, 1, tiles)
+    pull(0, 1)
+    push(0, 2)
     gather(1, 1 - (me & 1))
     push(1, 0)
+    pull(0, 2)
+    if bits > 3:
+        push(0, 3)
     gather(1, me & 1)
-    permute_own(0, 1)
-    pull(0, 1)
-    push(0, 2)
     pull(1, 0)
     push(1, 1)
-    permute_own(1, 2)
-
-    def finish(stream):
-        mine[stream] = acc[stream, me]
-        ka_copy(mine.at[stream], nextb.at[stream], 1 + stream).start()
-
-    for stage in range(2, bits):
+    for stage in range(3, bits):
         pull(0, stage)
         if stage + 1 < bits:
             push(0, stage + 1)
-        else:
-            finish(0)
-        pull(1, stage - 1)
-        push(1, stage)
+    finish(0)
+    permute_own(0, 2)
+    for stage in range(1, bits - 1):
+        pull(1, stage)
+        push(1, stage + 1)
     wave_copy.wait()
     def plane():
         a, b = received[0], received[1]
@@ -256,7 +261,7 @@
         return carry
 
     lax.fori_loop(0, n, fill, 0)
-    push, pull, bits = halving(n, me, *last)
+    push, pull, bits = halving(n, me, orders_of(n), *last)
     for stream in range(2):
         push(stream, 0)
     for stage in range(bits):
@@ -325,12 +330,9 @@
 def local(waves, projectors, projector_order, shift_map, charges, atom_phase):
     n = lax.axis_size("pw")
     kn = lax.axis_size("ka")
-    pw_dev = waves.shape[2]
     last_k = lax.axis_index("ka") == kn - 1
     pw_index = lax.axis_index("pw")
     inverse = invert(projector_order, projector_order.shape[0])
-    local_map = shift_map - pw_index * pw_dev
-    target = jnp.where(last_k, local_map, jnp.arange(pw_dev, dtype=jnp.int32))[None, :]
     atom_dev = atom_phase.shape[0] // n
     phase = lax.dynamic_slice_in_dim(atom_phase, pw_index * atom_dev, atom_dev)
     phase = jnp.where(last_k, phase, 0.0)
@@ -341,7 +343,7 @@
     sym = 0.5 * (raw + jnp.transpose(raw, (0, 2, 1)))
     eye = jnp.eye(atom_dev, dtype=jnp.float32)
     full = (sym[:, :, None, :] * eye[:, None, :, None]).reshape(atom_dev * PPA, atom_dev * PPA)
-    summed = fused(n, kn, inverse, target, cosine, sine, full, waves, projectors)
+    summed = fused(n, kn, inverse, shift_map[None, :], cosine, sine, full, waves, projectors)
     return jnp.transpose(summed, (1, 0, 2))[None]
 
 

time: 95 us -> 81.8 us (0.86)
  Pallas kernels: 84.8 us -> 72.9 us
  other arithmetic: 5.77 us -> 4.47 us
    pallas_call x1, Pallas kernels: 84.8 us -> 72.9 us  [fused(): pl.pallas_call(functools.partial(fused_kernel, n, kn), out_shape=jax.Shap...]
    select_n x1 -> x0, other arithmetic: 1.3 us -> none  [local(): jnp.where(last_k, local_map, jnp.arange(pw_dev, dtype=jnp.int32))[None, :]]
where the time goes in v3:
time: 81.8 us; the launch traced here: 81.6 us
  Pallas kernels  72.9 us (89%)
  other arithmetic  4.47 us (5%)
  local copies, waits for them, and re-layouts  4.14 us (5%)
    pallas_call x1, Pallas kernels, fused(): pl.pallas_call(functools.partial(fused_kernel, n, kn), out_shape=jax.Shap...  72.9 us
    reduce_sum x1, other arithmetic, invert(): return jnp.sum(jnp.where(order[None, :] == slot, place, 0), axis=1)  3.5 us

profile of v3, /device:TPU:0, one launch (start us, length us, event | category | flops | bytes accessed | tf_op | source)
XLA Modules:
  0.0 81.6 jit_solution(4050945757196173089)
XLA Ops:
  0.0 0.0 copy-start
  0.0 0.8 fusion.2
  0.8 0.1 broadcast_in_dim.27
  0.9 0.7 cos.16.cosine
  1.6 0.1 broadcast_in_dim.28
  1.7 0.7 sin.16.sine
  2.4 0.0 copy-done
  2.4 0.1 constant_dynamic-slice_fusion
  2.5 0.1 fusion
  2.6 0.2 copy.16
  2.8 0.1 broadcast_multiply_fusion
  2.9 0.9 %mul.33.sym = f32[144,144]{1,0:T(8,128)} reshape(f32[8,18,8,18]{3,2,1,0:T(8,128)S(1)} %broadcast_multiply_fusion) | data formatting | bytes 165888 | tf_op jit(solution)/shard_map/mul | solution.py:345
  3.7 3.5 %select_reduce_fusion.inverse = s32[2304]{0:T(1024)} fusion(s32[2304]{0:T(1024)} %param.8), kind=kLoop, calls=%fused_computation | loop fusion | flops 15922944 | bytes 18432 | tf_op jit(solution)/shard_map/reduce_sum | solution.py:327
  7.2 72.9 %shard_map.64 = f32[2,16,256]{2,1,0:T(8,128)} custom-call(s32[2304]{0:T(1024)} %select_reduce_fusion.inverse, s32[1,2048]{1,0:T(1,128)} %bitcast.11, f32[144,1]{1,0:T(8,128)} %cos.16.cosine, f32[144,1]{1,0:T(8,128)} %sin.16.sine, f32[144,144]{1,0:T(8,128)} %mul.33.sym, bf16[1,2,2048,256]{3,2,1,0:T(8,128)(2,1)} %wave_hbm.1, bf16[1,2,2048,2304]{3,2,1,0:T(8,128)(2,1)} %beta_hbm.1), custom_call_target="tpu_custom_call" | custom-call | tf_op jit(solution)/shard_map/pallas_call | solution.py:298
  80.2 1.4 %copy.19 = f32[1,16,2,256]{3,2,1,0:T(2,128)} copy(f32[1,16,2,256]{3,1,2,0:T(8,128)} %bitcast.10) | data formatting | bytes 65536 | tf_op jit(solution)/shard_map/broadcast_in_dim | solution.py:347
  (1 shorter events, 0.0 us)
Async XLA Ops:
  0.0 2.4 %copy-start = (f32[128,18,18]{0,2,1:T(8,128)S(1)}, f32[128,18,18]{0,2,1:T(8,128)}, u32[]{:S(2)}) copy-start(f32[128,18,18]{0,2,1:T(8,128)} %param.10) | copy-start | bytes 497668
